TPU v7x, 256 devices: a whole 4x4x8 slice. The times are simulated.
256 devices in a mesh: pw: 64 (over y_lo, z, x), atom: 4 (over y_hi, core).
Axes of the slice: x: 4, y: 4 (y_hi: 2, y_lo: 2; y = y_hi * 2 + y_lo), z: 8, core: 2. Of those that a mesh axis runs over, the one named last changes fastest.
Arguments:
- bands_in: float32 [2, 8, 32768], P(None, None, 'pw'), may hold values from -6 to 6
- template: bfloat16 [2, 64, 32768], P(None, None, 'pw'), may hold values from -0.03125 to 0.03125
- potential: bfloat16 [1024, 8192], P(('pw', 'atom')), may hold values from -0.5 to 0.5
- miller: int32 [3, 32768], P(None, 'pw'), may hold values from -32 to 32, as said below
- positions: float32 [3, 1024], replicated, may hold values from 0 to 1
- species: int32 [1024], replicated, may hold values from 0 to 1
- atom_order: int32 [1024], replicated, may hold values from 0 to 1023, each once
- reciprocal: float32 [3], replicated, may hold values from 0.03 to 0.1
Outputs:
- applied_once: float32 [2, 8, 32768], P(None, None, 'pw')
- applied_twice: float32 [2, 8, 32768], P(None, None, 'pw')
Inputs may be any that keep to these rules, and one draw needn't show every extreme that they name: `atom_order`: each atom stands in exactly one slot. `miller`: no two plane waves have the same triple of Miller indices; the triples (-32, -32, -32) and (32, 32, 32) are always among them.
All inputs are finite; a program needn't handle non-finite values.
Results may differ from a plain program's by a relative error of at most 0.005.
Values may be sent and summed in bfloat16 or wider, within the bound.
No kernel may reach another device: no remote copies, remote signals or barrier semaphores. Data moves between devices by JAX's collectives and lax.ppermute only.
A program may use at most 64 MiB of HBM per device.

v0:
```python
import math
import jax
import jax.numpy as jnp
from jax import lax
from jax.sharding import PartitionSpec as P

full_turn = 2.0 * math.pi


def phases(miller_real, centres):
    angles = full_turn * (
        centres[0][:, None] * miller_real[0][None, :]
        + centres[1][:, None] * miller_real[1][None, :]
        + centres[2][:, None] * miller_real[2][None, :]
    )
    return (jnp.cos(angles), jnp.sin(angles))


def project_block(template_flat, fields, cos_part, sin_part, chosen):
    band_count = fields.shape[1]
    real_wave = cos_part[:, None, :] * fields[0][None] - sin_part[:, None, :] * fields[1][None]
    imag_wave = sin_part[:, None, :] * fields[0][None] + cos_part[:, None, :] * fields[1][None]
    stacked = jnp.stack([real_wave, imag_wave], axis=1).astype(jnp.bfloat16)
    atom_count = stacked.shape[0]
    flattened = stacked.reshape(atom_count * 2 * band_count, stacked.shape[3])
    correlations = lax.dot_general(
        template_flat, flattened, (((1,), (1,)), ((), ())), preferred_element_type=jnp.float32
    )
    species_count = chosen.shape[1]
    harmonics = template_flat.shape[0] // species_count
    correlations = correlations.reshape(species_count, harmonics, atom_count, 2, band_count)
    accumulated = jnp.zeros((harmonics, atom_count, 2, band_count), jnp.float32)
    for species_id in range(species_count):
        accumulated = (
            accumulated + chosen[:, species_id][None, :, None, None] * correlations[species_id]
        )
    return jnp.transpose(accumulated, (1, 2, 0, 3))


def product(matrices, vectors):
    return jnp.einsum("alm,amb->alb", matrices, vectors, precision=lax.Precision.HIGHEST)


def apply_potential(potential, coeffs):
    atom_count = coeffs.shape[0]
    harmonics = coeffs.shape[2]
    matrices = potential.astype(jnp.float32).reshape(atom_count, 2, harmonics, harmonics)
    real_new = product(matrices[:, 0], coeffs[:, 0]) - product(matrices[:, 1], coeffs[:, 1])
    imag_new = product(matrices[:, 0], coeffs[:, 1]) + product(matrices[:, 1], coeffs[:, 0])
    return jnp.stack([real_new, imag_new], axis=1).astype(jnp.bfloat16)


def return_block(template_flat, applied, cos_part, sin_part, chosen):
    atom_count, _, harmonics, band_count = applied.shape
    species_count = chosen.shape[1]
    reordered = jnp.transpose(applied, (2, 0, 1, 3))
    selected = jnp.stack(
        [
            reordered * chosen[:, species_id][None, :, None, None].astype(jnp.bfloat16)
            for species_id in range(species_count)
        ]
    )
    selected = selected.reshape(species_count * harmonics, atom_count * 2 * band_count)
    images = lax.dot_general(
        selected, template_flat, (((0,), (0,)), ((), ())), preferred_element_type=jnp.float32
    )
    images = images.reshape(atom_count, 2, band_count, template_flat.shape[1])
    real_out = jnp.sum(
        cos_part[:, None, :] * images[:, 0] + sin_part[:, None, :] * images[:, 1], axis=0
    )
    imag_out = jnp.sum(
        cos_part[:, None, :] * images[:, 1] - sin_part[:, None, :] * images[:, 0], axis=0
    )
    return jnp.stack([real_out, imag_out])


def per_device(bands_in, template, potential, miller, positions, species, atom_order, reciprocal):
    pw_count = lax.axis_size("pw")
    group_count = lax.axis_size("atom")
    group_id = lax.axis_index("atom")
    slot_dev = potential.shape[0]
    per_group = slot_dev * pw_count
    species_count, harmonics, wave_count = template.shape
    band_count = bands_in.shape[1]
    template_flat = template.reshape(species_count * harmonics, wave_count)
    local_rows = jnp.arange(per_group, dtype=jnp.int32)
    slot_ids = (local_rows // slot_dev * group_count + group_id) * slot_dev + local_rows % slot_dev
    atoms_here = atom_order[slot_ids]
    centres = positions[:, atoms_here]
    kinds = species[atoms_here]
    chosen = (kinds[:, None] == jnp.arange(species_count, dtype=jnp.int32)[None, :]).astype(
        jnp.float32
    )
    miller_real = miller.astype(jnp.float32)
    kinetic = 0.5 * (
        (reciprocal[0] * miller_real[0]) ** 2
        + (reciprocal[1] * miller_real[1]) ** 2
        + (reciprocal[2] * miller_real[2]) ** 2
    )
    cos_all, sin_all = phases(miller_real, centres)
    block_size = math.gcd(per_group, 32)
    block_count = per_group // block_size
    row_width = 2 * harmonics * band_count

    def apply_once(fields):

        def projected(blocknum):
            first_row = blocknum * block_size
            chosen_part = lax.dynamic_slice_in_dim(chosen, first_row, block_size, 0)
            cos_part = lax.dynamic_slice_in_dim(cos_all, first_row, block_size, 0)
            sin_part = lax.dynamic_slice_in_dim(sin_all, first_row, block_size, 0)
            return project_block(template_flat, fields, cos_part, sin_part, chosen_part)

        coeffs = lax.map(projected, jnp.arange(block_count, dtype=jnp.int32)).reshape(
            per_group, row_width
        )
        summed = lax.psum(coeffs, "pw")
        segment = lax.all_gather(potential, "pw", axis=0, tiled=True)
        row_count = segment.shape[0]
        segment_coeffs = summed.reshape(row_count, 2, harmonics, band_count)
        applied = apply_potential(segment, segment_coeffs).reshape(row_count, row_width)
        applied = applied.reshape(per_group, 2, harmonics, band_count)

        def returned(blocknum, summed_up):
            first_row = (blocknum * block_size).astype(jnp.int32)
            chosen_part = lax.dynamic_slice_in_dim(chosen, first_row, block_size, 0)
            applied_part = lax.dynamic_slice_in_dim(applied, first_row, block_size, 0)
            cos_part = lax.dynamic_slice_in_dim(cos_all, first_row, block_size, 0)
            sin_part = lax.dynamic_slice_in_dim(sin_all, first_row, block_size, 0)
            return summed_up + return_block(
                template_flat, applied_part, cos_part, sin_part, chosen_part
            )

        summed_up = lax.fori_loop(
            0, block_count, returned, jnp.zeros((2, band_count, wave_count), jnp.float32)
        )
        return lax.psum(summed_up, "atom") + kinetic[None, None, :] * fields

    applied_once = apply_once(bands_in)
    applied_twice = apply_once(applied_once)
    return (applied_once, applied_twice)


def solution(mesh):
    in_specs = (
        P(None, None, "pw"),
        P(None, None, "pw"),
        P(("pw", "atom"), None),
        P(None, "pw"),
        P(),
        P(),
        P(),
        P(),
    )
    out_specs = (P(None, None, "pw"), P(None, None, "pw"))
    return jax.shard_map(
        per_device, mesh=mesh, in_specs=in_specs, out_specs=out_specs, check_vma=False
    )
```

profile of v0, /device:TPU:1, one launch (start us, length us, event | category | flops | bytes accessed | tf_op | source)
XLA Modules:
  0.0 1698.9 jit_solution(8377880044509035921)
XLA Ops:
  9.7 1.4 gather_fusion
  12.1 1.9 gather_fusion.2
  14.0 3.1 fusion.24
  17.4 25.3 %while.48 = (s32[]{:T(128)}, f32[8,32,2,64,8]{3,4,1,0,2:T(8,128)S(1)}, s32[8]{0:T(128)S(1)}, f32[256,2]{0,1:T(2,128)S(1)}, f32[256,512]{1,0:T(8,128)}, /*index=5...) while((s32[]{:T(128)}, ...), condition=%wide.region_1.2_spmd, body=%wide.region_0.1_spmd.sunk | while | flops 68517896 | bytes 4819139 | solution.py:114
  42.7 1.3 copy-done.4
  44.9 1.9 add_multiply_fusion.1
  46.9 224.9 %all-gather.3.cloned.1.call-done = bf16[64,4,8192]{2,1,0:T(4,128)(2,1)} async-done(((bf16[1,4,8192]{2,1,0:T(4,128)(2,1)}), bf16[64,4,8192]{2,1,0:T(4,128)(2,1)}) %all-gather.3.cloned.1.call-update) | async-done | bytes 4194320 | tf_op jit(solution)/shard_map/all_gather | solution.py:118
  271.8 13.4 reshape.268
  285.2 601.6 %all-reduce.3.cloned.1.call-done = f32[256,2,64,8]{2,3,0,1:T(8,128)} async-done(((f32[256,2,64,8]{2,3,0,1:T(8,128)}), f32[256,2,64,8]{2,3,0,1:T(8,128)}) %all-reduce.3.cloned.1.call-update) | async-done | bytes 1048592 | tf_op jit(solution)/shard_map/psum | solution.py:117
  886.7 8.6 fusion.6
  895.4 8.6 fusion.7
  904.0 6.6 fusion.21
  910.6 6.6 fusion.20
  917.4 16.8 while.50
  934.2 57.2 %psum.29 = f32[2,8,512]{2,1,0:T(8,128)S(1)} all-reduce(f32[2,8,512]{2,1,0:T(8,128)S(1)} %get-tuple-element.335), channel_id=1, replica_groups=mesh['pw'=64,'atom'=4] {'atom'}, use_global_device_ids=true, to_apply=%region_7.8 | all-reduce | flops 8192 | bytes 65536 | tf_op jit(solution)/shard_map/psum | solution.py:137
  991.6 25.3 %while.49 = (s32[]{:T(128)}, f32[8,32,2,64,8]{3,4,1,0,2:T(8,128)S(1)}, s32[8]{0:T(128)S(1)}, f32[256,2]{0,1:T(2,128)S(1)}, f32[256,512]{1,0:T(8,128)}, /*index=5...) while((s32[]{:T(128)}, ...), condition=%wide.region_9.10_spmd, body=%wide.region_8.9_spmd.sunk | while | flops 68517896 | bytes 4819139 | solution.py:114
  1017.0 1.3 copy-done.3
  1018.3 567.7 %all-reduce.5.cloned.1.call-done = f32[256,2,64,8]{2,3,0,1:T(8,128)} async-done(((f32[256,2,64,8]{2,3,0,1:T(8,128)}), f32[256,2,64,8]{2,3,0,1:T(8,128)}) %all-reduce.5.cloned.1.call-update) | async-done | bytes 1048592 | tf_op jit(solution)/shard_map/psum | solution.py:117
  1586.1 8.6 fusion.4
  1594.7 8.5 fusion.5
  1603.2 8.3 fusion.23
  1611.5 6.6 fusion.22
  1618.4 16.8 while.51
  1635.1 56.6 %psum.31 = f32[2,8,512]{2,1,0:T(8,128)S(1)} all-reduce(f32[2,8,512]{2,1,0:T(8,128)S(1)} %get-tuple-element.337), channel_id=1, replica_groups=mesh['pw'=64,'atom'=4] {'atom'}, use_global_device_ids=true, to_apply=%region_15.16 | all-reduce | flops 8192 | bytes 65536 | tf_op jit(solution)/shard_map/psum | solution.py:137
  (403 shorter events, 77.2 us)
Async XLA Ops:
  7.2 2.5 copy-start
  7.2 10.1 copy-start.8
  7.2 10.1 copy-start.2
  7.2 264.6 %all-gather.3.cloned.1.call-start = ((), (), s32[]{:S(2)}) async-start(), calls=%async_computation.2 | async-start | bytes 4259840 | tf_op jit(solution)/shard_map/all_gather | solution.py:118
  7.9 878.8 %all-reduce.3.cloned.1.call-start = ((), (), s32[]{:S(2)}) async-start(), calls=%async_computation | async-start | bytes 4194304 | tf_op jit(solution)/shard_map/psum | solution.py:117
  17.3 26.9 %copy-start.9 = (f32[3]{0:T(128)S(1)}, f32[3]{0:T(128)}, u32[]{:S(2)}) copy-start(f32[3]{0:T(128)} %param.23) | copy-start | bytes 40
  42.7 1.3 copy-start.4
  44.0 1542.0 %all-reduce.5.cloned.1.call-start = ((), (), s32[]{:S(2)}) async-start(), calls=%async_computation.1 | async-start | bytes 4194304 | tf_op jit(solution)/shard_map/psum | solution.py:117
  886.7 17.3 %copy-start.1 = (bf16[256,2,64,64]{3,2,1,0:T(8,128)(2,1)S(1)}, bf16[256,2,64,64]{3,2,1,0:T(8,128)(2,1)}, u32[]{:S(2)}) copy-start(bf16[256,2,64,64]{3,2,1,0:T(8,128)(2,1)} %reshape.268) | copy-start | bytes 12582916
  895.3 8.6 copy-start.5
  1016.9 1.3 copy-start.3
  1017.0 674.8 %copy-start.7 = (f32[2,8,512]{2,1,0:T(8,128)}, f32[2,8,512]{2,1,0:T(8,128)S(1)}, u32[]{:S(2)}) copy-start(f32[2,8,512]{2,1,0:T(8,128)S(1)} %get-tuple-element.947) | copy-start | bytes 98308
  1586.1 8.6 copy-start.6
  1586.1 25.4 %slice-start = ((s8[8388608]{0:T(1024)(128)(4,1)}), s8[4194304]{0:T(1024)(128)(4,1)S(1)}, s32[]{:S(2)}) async-start(s8[8388608]{0:T(1024)(128)(4,1)} %bitcast.282), calls=%async_computation.3 | async-start | bytes 8388608
  1594.7 16.8 slice-start.1
Sparse Core Ops, SparseCore 0:
  9.8 261.9 all-gather.2
  274.4 612.2 all-reduce.2
  1018.4 567.5 all-reduce.4
where the time goes:
time: 1700 us
  waiting for transfers between devices  1390 us (82%)
  blocking collectives  114 us (7%)
  local copies, waits for them, and re-layouts  73.1 us (4%)
  matrix products  71.7 us (4%)
  other arithmetic  18.1 us (1%)
    psum x2, waiting for transfers between devices, apply_once(): summed = lax.psum(coeffs, 'pw')  1170 us
    all_gather x1, waiting for transfers between devices, apply_once(): segment = lax.all_gather(potential, 'pw', axis=0, tiled=True)  225 us
    psum x2, blocking collectives, apply_once(): return lax.psum(summed_up, 'atom') + kinetic[None, None, :] * fields  114 us
    dot_general x8, matrix products, product(): jnp.einsum('alm,amb->alb', matrices, vectors, precision=lax.Precision.HIG...  62.5 us
  transfers between devices with their start and end apart: 3, of which 3 were waited for; matrix products, arithmetic and copies ran while one was open for 3% of the time, Pallas kernels for 0%

commit v1 on v0

--- a/solution.py
+++ b/solution.py
@@ -115,7 +115,9 @@
             per_group, row_width
         )
         summed = lax.psum(coeffs, "pw")
-        segment = lax.all_gather(potential, "pw", axis=0, tiled=True)
+        segment = jnp.concatenate(
+            lax.all_to_all(jnp.stack([potential] * lax.axis_size("pw")), "pw", 0, 0), axis=0
+        )
         row_count = segment.shape[0]
         segment_coeffs = summed.reshape(row_count, 2, harmonics, band_count)
         applied = apply_potential(segment, segment_coeffs).reshape(row_count, row_width)

time: 1700 us -> 1450 us (0.85)
  waiting for transfers between devices: 1390 us -> 1130 us
    all_gather x1 -> x0, waiting for transfers between devices: 225 us -> none  [apply_once(): segment = lax.all_gather(potential, 'pw', axis=0, tiled=True)]
    psum x2, waiting for transfers between devices: 1170 us -> 1070 us  [apply_once(): summed = lax.psum(coeffs, 'pw')]
    all_to_all x0 -> x1, waiting for transfers between devices: none -> 55.9 us  [apply_once(): lax.all_to_all(jnp.stack([potential] * lax.axis_size('pw')), 'pw', 0, 0)]
where the time goes in v1:
time: 1450 us
  waiting for transfers between devices  1130 us (78%)
  blocking collectives  114 us (8%)
  local copies, waits for them, and re-layouts  76.6 us (5%)
  matrix products  71.8 us (5%)
  other arithmetic  17.4 us (1%)
    psum x2, waiting for transfers between devices, apply_once(): summed = lax.psum(coeffs, 'pw')  1070 us
    psum x2, blocking collectives, apply_once(): return lax.psum(summed_up, 'atom') + kinetic[None, None, :] * fields  114 us
    dot_general x8, matrix products, product(): jnp.einsum('alm,amb->alb', matrices, vectors, precision=lax.Precision.HIG...  62.5 us
    all_to_all x1, waiting for transfers between devices, apply_once(): lax.all_to_all(jnp.stack([potential] * lax.axis_size('pw')), 'pw', 0, 0)  55.9 us
  transfers between devices with their start and end apart: 3, of which 3 were waited for; matrix products, arithmetic and copies ran while one was open for 3% of the time, Pallas kernels for 0%

profile of v1, /device:TPU:1, one launch (start us, length us, event | category | flops | bytes accessed | tf_op | source)
XLA Modules:
  0.0 1447.9 jit_solution(13912880028599967163)
XLA Ops:
  7.2 4.8 stack.110
  12.0 13.9 all-to-all-start
  26.3 1.4 gather_fusion
  28.7 1.4 gather_fusion.2
  30.1 3.1 fusion.24
  33.4 25.3 %while.48 = (s32[]{:T(128)}, f32[8,32,2,64,8]{3,4,1,0,2:T(8,128)S(1)}, s32[8]{0:T(128)S(1)}, f32[256,2]{0,1:T(2,128)S(1)}, f32[256,512]{1,0:T(8,128)}, /*index=5...) while((s32[]{:T(128)}, ...), condition=%wide.region_1.2_spmd, body=%wide.region_0.1_spmd.sunk | while | flops 68517896 | bytes 4819139 | solution.py:114
  61.0 1.9 add_multiply_fusion.1
  62.9 55.9 %all-to-all-done = bf16[64,4,8192]{2,1,0:T(4,128)(2,1)} async-done(((bf16[64,4,8192]{2,1,0:T(4,128)(2,1)}), bf16[64,4,8192]{2,1,0:T(4,128)(2,1)}, u32[]{:S(2)}, u32[]{:S(2)}) %all-to-all-start) | async-done | bytes 4194336 | tf_op jit(solution)/shard_map/all_to_all | solution.py:119
  118.9 13.4 reshape.273
  132.3 503.1 %all-reduce.3.cloned.1.call-done = f32[256,2,64,8]{2,3,0,1:T(8,128)} async-done(((f32[256,2,64,8]{2,3,0,1:T(8,128)}), f32[256,2,64,8]{2,3,0,1:T(8,128)}) %all-reduce.3.cloned.1.call-update) | async-done | bytes 1048592 | tf_op jit(solution)/shard_map/psum | solution.py:117
  635.4 8.6 fusion.6
  644.0 8.6 fusion.7
  652.7 6.6 fusion.21
  659.3 6.6 fusion.20
  666.1 16.8 %while.50 = (s32[]{:T(128)}, f32[2,8,512]{2,1,0:T(8,128)S(1)}, f32[256,512]{1,0:T(8,128)}, bf16[256,2,64,8]{2,3,0,1:T(8,128)(2,1)S(1)}, bf16[256,2]{0,1:T(2,128)...) while((s32[]{:T(128)}, f32[2,8,512]{2,1,0:T(8,128)S(1)}, ...), condition=%wide.region_6.7_spmd.clone, body=%wide.region_3.6_spmd.clone.sunk | while | flops 68468744 | bytes 3933881 | solution.py:136
  682.9 57.2 %psum.29 = f32[2,8,512]{2,1,0:T(8,128)S(1)} all-reduce(f32[2,8,512]{2,1,0:T(8,128)S(1)} %get-tuple-element.335), channel_id=1, replica_groups=mesh['pw'=64,'atom'=4] {'atom'}, use_global_device_ids=true, to_apply=%region_7.8 | all-reduce | flops 8192 | bytes 65536 | tf_op jit(solution)/shard_map/psum | solution.py:139
  740.3 25.3 %while.49 = (s32[]{:T(128)}, f32[8,32,2,64,8]{3,4,1,0,2:T(8,128)S(1)}, s32[8]{0:T(128)S(1)}, f32[256,2]{0,1:T(2,128)S(1)}, f32[256,512]{1,0:T(8,128)}, /*index=5...) while((s32[]{:T(128)}, ...), condition=%wide.region_9.10_spmd, body=%wide.region_8.9_spmd.sunk | while | flops 68517896 | bytes 4819139 | solution.py:114
  767.0 567.8 %all-reduce.5.cloned.1.call-done = f32[256,2,64,8]{2,3,0,1:T(8,128)} async-done(((f32[256,2,64,8]{2,3,0,1:T(8,128)}), f32[256,2,64,8]{2,3,0,1:T(8,128)}) %all-reduce.5.cloned.1.call-update) | async-done | bytes 1048592 | tf_op jit(solution)/shard_map/psum | solution.py:117
  1334.8 8.6 fusion.4
  1343.4 8.5 fusion.5
  1351.9 8.3 fusion.23
  1360.2 6.6 fusion.22
  1367.1 16.8 %while.51 = (s32[]{:T(128)}, f32[2,8,512]{2,1,0:T(8,128)S(1)}, f32[256,512]{1,0:T(8,128)}, bf16[256,2,64,8]{2,3,0,1:T(8,128)(2,1)S(1)}, bf16[256,2]{0,1:T(2,128)...) while((s32[]{:T(128)}, f32[2,8,512]{2,1,0:T(8,128)S(1)}, ...), condition=%wide.region_14.15_spmd.clone, body=%wide.region_11.14_spmd.clone.sunk | while | flops 68468744 | bytes 3933881 | solution.py:136
  1383.9 56.6 %psum.31 = f32[2,8,512]{2,1,0:T(8,128)S(1)} all-reduce(f32[2,8,512]{2,1,0:T(8,128)S(1)} %get-tuple-element.337), channel_id=1, replica_groups=mesh['pw'=64,'atom'=4] {'atom'}, use_global_device_ids=true, to_apply=%region_15.16 | all-reduce | flops 8192 | bytes 65536 | tf_op jit(solution)/shard_map/psum | solution.py:139
  (409 shorter events, 77.6 us)
Async XLA Ops:
  7.2 19.1 %copy-start = (s32[1024]{0:T(1024)S(1)}, s32[1024]{0:T(1024)}, u32[]{:S(2)}) copy-start(s32[1024]{0:T(1024)} %param.22) | copy-start | bytes 12292
  12.0 14.0 copy-start.11
  12.0 14.0 copy-start.10
  12.0 16.7 %copy-start.1 = (s32[1024]{0:T(1024)S(1)}, s32[1024]{0:T(1024)}, u32[]{:S(2)}) copy-start(s32[1024]{0:T(1024)} %param.21) | copy-start | bytes 12292
  12.0 106.9 %all-to-all-start = ((bf16[64,4,8192]{2,1,0:T(4,128)(2,1)}), bf16[64,4,8192]{2,1,0:T(4,128)(2,1)}, u32[]{:S(2)}, u32[]{:S(2)}) async-start(bf16[64,4,8192]{2,1,0:T(4,128)(2,1)} %stack.110), calls=%async_computation | async-start | bytes 8388608 | tf_op jit(solution)/shard_map/all_to_all | solution.py:119
  25.9 7.5 copy-start.3
  25.9 7.5 copy-start.9
  25.9 609.5 %all-reduce.3.cloned.1.call-start = ((), (), s32[]{:S(2)}) async-start(), calls=%async_computation.1 | async-start | bytes 4194304 | tf_op jit(solution)/shard_map/psum | solution.py:117
  33.4 26.9 %copy-start.12 = (f32[3]{0:T(128)S(1)}, f32[3]{0:T(128)}, u32[]{:S(2)}) copy-start(f32[3]{0:T(128)} %param.23) | copy-start | bytes 40
  58.7 1.3 copy-start.5
  60.1 1274.7 %all-reduce.5.cloned.1.call-start = ((), (), s32[]{:S(2)}) async-start(), calls=%async_computation.2 | async-start | bytes 4194304 | tf_op jit(solution)/shard_map/psum | solution.py:117
  635.4 17.3 %copy-start.2 = (bf16[256,2,64,64]{3,2,1,0:T(8,128)(2,1)S(1)}, bf16[256,2,64,64]{3,2,1,0:T(8,128)(2,1)}, u32[]{:S(2)}) copy-start(bf16[256,2,64,64]{3,2,1,0:T(8,128)(2,1)} %reshape.273) | copy-start | bytes 12582916
  644.0 8.6 copy-start.6
  765.6 1.3 copy-start.4
  765.6 674.8 %copy-start.8 = (f32[2,8,512]{2,1,0:T(8,128)}, f32[2,8,512]{2,1,0:T(8,128)S(1)}, u32[]{:S(2)}) copy-start(f32[2,8,512]{2,1,0:T(8,128)S(1)} %get-tuple-element.933) | copy-start | bytes 98308
  1334.8 8.6 copy-start.7
  1334.8 25.4 %slice-start = ((s8[8388608]{0:T(1024)(128)(4,1)}), s8[4194304]{0:T(1024)(128)(4,1)S(1)}, s32[]{:S(2)}) async-start(s8[8388608]{0:T(1024)(128)(4,1)} %bitcast.281), calls=%async_computation.3 | async-start | bytes 8388608
  1343.4 16.8 %slice-start.1 = ((s8[8388608]{0:T(1024)(128)(4,1)}), s8[4194304]{0:T(1024)(128)(4,1)S(1)}, s32[]{:S(2)}) async-start(s8[8388608]{0:T(1024)(128)(4,1)} %bitcast.281), calls=%async_computation.4 | async-start | bytes 8388608
Sparse Core Ops, SparseCore 0:
  60.2 575.1 all-reduce.2
  767.1 567.6 all-reduce.4

commit v2 on v0

--- a/solution.py
+++ b/solution.py
@@ -134,7 +134,7 @@
         summed_up = lax.fori_loop(
             0, block_count, returned, jnp.zeros((2, band_count, wave_count), jnp.float32)
         )
-        return lax.psum(summed_up, "atom") + kinetic[None, None, :] * fields
+        return jnp.sum(lax.all_gather(summed_up, "atom"), axis=0) + kinetic[None, None, :] * fields
 
     applied_once = apply_once(bands_in)
     applied_twice = apply_once(applied_once)

time: 1700 us -> 1690 us (level)
    psum x2 -> x0, blocking collectives: 114 us -> none  [apply_once(): return lax.psum(summed_up, 'atom') + kinetic[None, None, :] * fields]
    all_gather x0 -> x2, blocking collectives: none -> 102 us  [apply_once(): lax.all_gather(summed_up, 'atom')]
where the time goes in v2:
time: 1690 us
  waiting for transfers between devices  1390 us (82%)
  blocking collectives  102 us (6%)
  local copies, waits for them, and re-layouts  73.1 us (4%)
  matrix products  71.7 us (4%)
  other arithmetic  18.1 us (1%)
    psum x2, waiting for transfers between devices, apply_once(): summed = lax.psum(coeffs, 'pw')  1170 us
    all_gather x1, waiting for transfers between devices, apply_once(): segment = lax.all_gather(potential, 'pw', axis=0, tiled=True)  225 us
    all_gather x2, blocking collectives, apply_once(): lax.all_gather(summed_up, 'atom')  102 us
    dot_general x8, matrix products, product(): jnp.einsum('alm,amb->alb', matrices, vectors, precision=lax.Precision.HIG...  62.5 us
  transfers between devices with their start and end apart: 3, of which 3 were waited for; matrix products, arithmetic and copies ran while one was open for 3% of the time, Pallas kernels for 0%

profile of v2, /device:TPU:1, one launch (start us, length us, event | category | flops | bytes accessed | tf_op | source)
XLA Modules:
  0.0 1686.8 jit_solution(5782890927761317548)
XLA Ops:
  9.7 1.4 gather_fusion
  12.1 1.9 gather_fusion.2
  14.0 3.1 fusion.24
  17.4 25.3 %while.48 = (s32[]{:T(128)}, f32[8,32,2,64,8]{3,4,1,0,2:T(8,128)S(1)}, s32[8]{0:T(128)S(1)}, f32[256,2]{0,1:T(2,128)S(1)}, f32[256,512]{1,0:T(8,128)}, /*index=5...) while((s32[]{:T(128)}, ...), condition=%wide.region_1.2_spmd, body=%wide.region_0.1_spmd.sunk | while | flops 68517896 | bytes 4819139 | solution.py:114
  42.7 1.3 copy-done.3
  44.9 1.9 add_multiply_fusion.1
  46.9 224.9 %all-gather.5.cloned.1.call-done = bf16[64,4,8192]{2,1,0:T(4,128)(2,1)} async-done(((bf16[1,4,8192]{2,1,0:T(4,128)(2,1)}), bf16[64,4,8192]{2,1,0:T(4,128)(2,1)}) %all-gather.5.cloned.1.call-update) | async-done | bytes 4194320 | tf_op jit(solution)/shard_map/all_gather | solution.py:118
  271.8 13.4 reshape.268
  285.2 601.6 %all-reduce.3.cloned.1.call-done = f32[256,2,64,8]{2,3,0,1:T(8,128)} async-done(((f32[256,2,64,8]{2,3,0,1:T(8,128)}), f32[256,2,64,8]{2,3,0,1:T(8,128)}) %all-reduce.3.cloned.1.call-update) | async-done | bytes 1048592 | tf_op jit(solution)/shard_map/psum | solution.py:117
  886.7 8.6 fusion.6
  895.4 8.6 fusion.7
  904.0 6.6 fusion.21
  910.6 6.6 fusion.20
  917.4 16.8 while.50
  934.2 51.1 %all-gather = f32[8,8,512]{2,1,0:T(8,128)S(1)} all-gather(f32[2,8,512]{2,1,0:T(8,128)S(1)} %get-tuple-element.335), channel_id=2, replica_groups=mesh['pw'=64,'atom'=4] {'atom'}, dimensions={0}, use_global_device_ids=true | all-gather | bytes 163840 | tf_op jit(solution)/shard_map/all_gather | solution.py:137
  985.5 25.3 %while.49 = (s32[]{:T(128)}, f32[8,32,2,64,8]{3,4,1,0,2:T(8,128)S(1)}, s32[8]{0:T(128)S(1)}, f32[256,2]{0,1:T(2,128)S(1)}, f32[256,512]{1,0:T(8,128)}, /*index=5...) while((s32[]{:T(128)}, ...), condition=%wide.region_9.10_spmd, body=%wide.region_8.9_spmd.sunk | while | flops 68517896 | bytes 4819139 | solution.py:114
  1010.8 1.3 copy-done.4
  1012.2 567.5 %all-reduce.5.cloned.1.call-done = f32[256,2,64,8]{2,3,0,1:T(8,128)} async-done(((f32[256,2,64,8]{2,3,0,1:T(8,128)}), f32[256,2,64,8]{2,3,0,1:T(8,128)}) %all-reduce.5.cloned.1.call-update) | async-done | bytes 1048592 | tf_op jit(solution)/shard_map/psum | solution.py:117
  1579.7 8.6 fusion.4
  1588.4 8.5 fusion.5
  1596.8 8.3 fusion.23
  1605.2 6.6 fusion.22
  1612.0 16.8 while.51
  1628.8 50.8 %all-gather.1 = f32[8,8,512]{2,1,0:T(8,128)S(1)} all-gather(f32[2,8,512]{2,1,0:T(8,128)S(1)} %get-tuple-element.337), channel_id=3, replica_groups=mesh['pw'=64,'atom'=4] {'atom'}, dimensions={0}, use_global_device_ids=true | all-gather | bytes 163840 | tf_op jit(solution)/shard_map/all_gather | solution.py:137
  (405 shorter events, 77.2 us)
Async XLA Ops:
  7.2 2.5 copy-start
  7.2 10.1 copy-start.8
  7.2 10.1 copy-start.2
  7.2 264.6 %all-gather.5.cloned.1.call-start = ((), (), s32[]{:S(2)}) async-start(), calls=%async_computation.2 | async-start | bytes 4259840 | tf_op jit(solution)/shard_map/all_gather | solution.py:118
  7.9 878.8 %all-reduce.3.cloned.1.call-start = ((), (), s32[]{:S(2)}) async-start(), calls=%async_computation | async-start | bytes 4194304 | tf_op jit(solution)/shard_map/psum | solution.py:117
  17.3 26.9 %copy-start.9 = (f32[3]{0:T(128)S(1)}, f32[3]{0:T(128)}, u32[]{:S(2)}) copy-start(f32[3]{0:T(128)} %param.23) | copy-start | bytes 40
  42.7 1.3 copy-start.3
  44.0 1535.7 %all-reduce.5.cloned.1.call-start = ((), (), s32[]{:S(2)}) async-start(), calls=%async_computation.1 | async-start | bytes 4194304 | tf_op jit(solution)/shard_map/psum | solution.py:117
  886.7 17.3 %copy-start.1 = (bf16[256,2,64,64]{3,2,1,0:T(8,128)(2,1)S(1)}, bf16[256,2,64,64]{3,2,1,0:T(8,128)(2,1)}, u32[]{:S(2)}) copy-start(bf16[256,2,64,64]{3,2,1,0:T(8,128)(2,1)} %reshape.268) | copy-start | bytes 12582916
  895.3 8.6 copy-start.5
  1010.8 1.3 copy-start.4
  1010.8 668.8 %copy-start.7 = (f32[2,8,512]{2,1,0:T(8,128)}, f32[2,8,512]{2,1,0:T(8,128)S(1)}, u32[]{:S(2)}) copy-start(f32[2,8,512]{2,1,0:T(8,128)S(1)} %get-tuple-element.947) | copy-start | bytes 98308
  1579.7 8.6 copy-start.6
  1579.7 25.4 %slice-start = ((s8[8388608]{0:T(1024)(128)(4,1)}), s8[4194304]{0:T(1024)(128)(4,1)S(1)}, s32[]{:S(2)}) async-start(s8[8388608]{0:T(1024)(128)(4,1)} %bitcast.284), calls=%async_computation.3 | async-start | bytes 8388608
  1588.4 16.8 slice-start.1
Sparse Core Ops, SparseCore 0:
  9.8 261.9 all-gather.4
  274.4 612.2 all-reduce.2
  1012.3 567.3 all-reduce.4
